TPU v7x, 32 devices: a whole 2x2x4 slice. The times are simulated.
32 devices in a mesh: dp: 8 (over z, core), tensor: 4 (over y, x).
Axes of the slice: x: 2, y: 2, z: 4, core: 2. Of those that a mesh axis runs over, the one named last changes fastest.
Arguments:
- tokens: bfloat16 [16384, 1152], P(('dp', 'tensor')), may hold values from -6 to 6
- norm_gains: float32 [2, 1152], P(None, ('dp', 'tensor')), may hold values from 0.5 to 1.5
- row_biases: float32 [4, 1152], P(None, ('dp', 'tensor')), may hold values from -3 to 3
- w_qkv: bfloat16 [3, 1152, 1152], P(None, 'dp', 'tensor'), may hold values from -1 to 1
- head_bias: float32 [2, 1152], P(None, 'tensor'), may hold values from -3 to 3
- w_out: bfloat16 [1152, 1152], P('tensor', 'dp'), may hold values from -1.5 to 1.5
- w_fc1: bfloat16 [1152, 4304], P('dp', 'tensor'), may hold values from -0.1875 to 0.1875
- fc1_bias: float32 [4304], P('tensor'), may hold values from -3 to 3
- w_fc2: bfloat16 [4304, 1152], P('tensor', 'dp'), may hold values from -0.09375 to 0.09375
- cotangent: bfloat16 [16384, 1152], P(('dp', 'tensor')), may hold values from -6 to 6
Outputs:
- output: float32 [16384, 1152], P(('dp', 'tensor'))
- grad_tokens: float32 [16384, 1152], P(('dp', 'tensor'))
- grad_norm_gains: float32 [2, 1152], P(None, ('dp', 'tensor'))
- grad_row_biases: float32 [4, 1152], P(None, ('dp', 'tensor'))
- grad_w_qkv: float32 [3, 1152, 1152], P(None, 'dp', 'tensor')
- grad_head_bias: float32 [2, 1152], P(None, 'tensor')
- grad_w_out: float32 [1152, 1152], P('tensor', 'dp')
- grad_w_fc1: float32 [1152, 4304], P('dp', 'tensor')
- grad_fc1_bias: float32 [4304], P('tensor')
- grad_w_fc2: float32 [4304, 1152], P('tensor', 'dp')
All inputs are finite; a program needn't handle non-finite values.
Results may differ from a plain program's by a relative error of at most 0.04.
Values may be sent and summed in bfloat16 or wider, within the bound.
No kernel may reach another device: no remote copies, remote signals or barrier semaphores. Data moves between devices by JAX's collectives and lax.ppermute only.
A program may use at most 192 MiB of HBM per device.

v0:
```python
import jax
import jax.numpy as jnp
from jax import lax
from jax.sharding import PartitionSpec as P

HD = 72
SEQ = 256
EPS = 1e-06


def norm_rows(values, gain_row, shifts):
    center = values - jnp.mean(values, axis=-1, keepdims=True)
    spread = lax.rsqrt(jnp.mean(center * center, axis=-1, keepdims=True) + EPS)
    normed = center * spread
    return (normed * gain_row + shifts, normed, spread)


def norm_back(grad_rows, normed, spread, gain_row):
    scaled = grad_rows * gain_row
    return spread * (
        scaled
        - jnp.mean(scaled, axis=-1, keepdims=True)
        - normed * jnp.mean(scaled * normed, axis=-1, keepdims=True)
    )


def gelu_tanh(pre_act):
    return jax.nn.gelu(pre_act, approximate=True)


def image_block(image_total):
    block_size = min(image_total, max(1, 512 // SEQ))
    while image_total % block_size:
        block_size = block_size - 1
    return block_size


def attend(block_in):
    query_b, keys_b, vals_b = block_in
    scores = jnp.einsum("gqhe,gkhe->ghqk", query_b, keys_b, preferred_element_type=jnp.float32)
    top_score = jnp.max(scores, axis=-1, keepdims=True)
    log_norm = top_score + jnp.log(jnp.sum(jnp.exp(scores - top_score), axis=-1, keepdims=True))
    probs_b = jnp.exp(scores - log_norm).astype(jnp.bfloat16)
    mixed = jnp.einsum(
        "ghqk,gkhe->gqhe", probs_b, vals_b, preferred_element_type=jnp.float32
    ).astype(jnp.bfloat16)
    return (mixed, log_norm[..., 0])


def attend_back(block_in):
    query_b, keys_b, vals_b, grad_b, log_norm = block_in
    scores = jnp.einsum("gqhe,gkhe->ghqk", query_b, keys_b, preferred_element_type=jnp.float32)
    probs_f = jnp.exp(scores - log_norm[..., None])
    probs_b = probs_f.astype(jnp.bfloat16)
    grad_vals = jnp.einsum("ghqk,gqhe->gkhe", probs_b, grad_b, preferred_element_type=jnp.float32)
    grad_probs = jnp.einsum("gqhe,gkhe->ghqk", grad_b, vals_b, preferred_element_type=jnp.float32)
    grad_scores = probs_f * (grad_probs - jnp.sum(probs_f * grad_probs, axis=-1, keepdims=True))
    grad_scores_b = grad_scores.astype(jnp.bfloat16)
    grad_query = jnp.einsum(
        "ghqk,gkhe->gqhe", grad_scores_b, keys_b, preferred_element_type=jnp.float32
    ) * HD ** (-0.5)
    grad_keys = jnp.einsum(
        "ghqk,gqhe->gkhe", grad_scores_b, query_b, preferred_element_type=jnp.float32
    )
    return (grad_query, grad_keys, grad_vals)


def body(
    tokens, norm_gains, row_biases, w_qkv, head_bias, w_out, w_fc1, fc1_bias, w_fc2, cotangent
):
    inv_root = HD ** (-0.5)
    gain_rows, shifts = (
        lax.all_gather(norm_gains, ("dp", "tensor"), axis=1, tiled=True),
        lax.all_gather(row_biases, ("dp", "tensor"), axis=1, tiled=True),
    )
    qkv_full, out_full, fc1_full, fc2_full = (
        lax.all_gather(w_qkv, "dp", axis=1, tiled=True),
        lax.all_gather(w_out, "dp", axis=1, tiled=True),
        lax.all_gather(w_fc1, "dp", axis=0, tiled=True),
        lax.all_gather(w_fc2, "dp", axis=1, tiled=True),
    )
    inputs_f = tokens.astype(jnp.float32)
    first_f, normed_one, spread_one = norm_rows(inputs_f, gain_rows[0], shifts[0])
    first_in, cot_all = (
        lax.all_gather(first_f.astype(jnp.bfloat16), "tensor", axis=0, tiled=True),
        lax.all_gather(cotangent, "tensor", axis=0, tiled=True),
    )
    group_rows = first_in.shape[0]
    images = group_rows // SEQ
    local_width = w_qkv.shape[2]
    local_heads = local_width // HD
    block_size = image_block(images)

    def to_blocks(array_in):
        return array_in.reshape(images // block_size, block_size, SEQ, local_heads, HD)

    query_rows = (
        (jnp.dot(first_in, qkv_full[0], preferred_element_type=jnp.float32) + head_bias[0])
        * inv_root
    ).astype(jnp.bfloat16)
    keys_rows = jnp.dot(first_in, qkv_full[1], preferred_element_type=jnp.float32).astype(
        jnp.bfloat16
    )
    vals_rows = (
        jnp.dot(first_in, qkv_full[2], preferred_element_type=jnp.float32) + head_bias[1]
    ).astype(jnp.bfloat16)
    query_blocks = to_blocks(query_rows)
    keys_blocks = to_blocks(keys_rows)
    vals_blocks = to_blocks(vals_rows)
    mixed_blocks, log_norm = lax.map(attend, (query_blocks, keys_blocks, vals_blocks))
    mixed = mixed_blocks.reshape(group_rows, local_width)
    attention = lax.psum_scatter(
        jnp.dot(mixed, out_full, preferred_element_type=jnp.float32).astype(jnp.bfloat16),
        "tensor",
        scatter_dimension=0,
        tiled=True,
    ).astype(jnp.float32)
    hidden_one = inputs_f + attention + shifts[1]
    second_f, normed_two, spread_two = norm_rows(hidden_one, gain_rows[1], shifts[2])
    second_in = lax.all_gather(second_f.astype(jnp.bfloat16), "tensor", axis=0, tiled=True)
    pre_act = jnp.dot(second_in, fc1_full, preferred_element_type=jnp.float32) + fc1_bias
    act_out, gelu_back = jax.vjp(gelu_tanh, pre_act)
    act_in = act_out.astype(jnp.bfloat16)
    mlp_out = lax.psum_scatter(
        jnp.dot(act_in, fc2_full, preferred_element_type=jnp.float32).astype(jnp.bfloat16),
        "tensor",
        scatter_dimension=0,
        tiled=True,
    ).astype(jnp.float32)
    output = hidden_one + mlp_out + shifts[3]
    cot_f = cotangent.astype(jnp.float32)
    grad_fc2 = jnp.dot(act_in.T, cot_all, preferred_element_type=jnp.float32)
    grad_act = jnp.dot(cot_all, fc2_full.T, preferred_element_type=jnp.float32)
    grad_pre = gelu_back(grad_act)[0]
    grad_fc1_bias = jnp.sum(grad_pre, axis=0)
    grad_pre_in = grad_pre.astype(jnp.bfloat16)
    grad_fc1 = jnp.dot(second_in.T, grad_pre_in, preferred_element_type=jnp.float32)
    grad_second = lax.psum_scatter(
        jnp.dot(grad_pre_in, fc1_full.T, preferred_element_type=jnp.float32).astype(jnp.bfloat16),
        "tensor",
        scatter_dimension=0,
        tiled=True,
    ).astype(jnp.float32)
    gain_two = jnp.sum(grad_second * normed_two, axis=0)
    shift_two = jnp.sum(grad_second, axis=0)
    grad_hidden = cot_f + norm_back(grad_second, normed_two, spread_two, gain_rows[1])
    shift_out = jnp.sum(grad_hidden, axis=0)
    shift_fc2 = jnp.sum(cot_f, axis=0)
    grad_hidden_in = grad_hidden.astype(jnp.bfloat16)
    grad_hidden_all = lax.all_gather(grad_hidden_in, "tensor", axis=0, tiled=True)
    grad_wout = jnp.dot(mixed.T, grad_hidden_all, preferred_element_type=jnp.float32)
    grad_mixed = jnp.dot(grad_hidden_all, out_full.T, preferred_element_type=jnp.float32).astype(
        jnp.bfloat16
    )
    grad_query, grad_keys, grad_vals = lax.map(
        attend_back, (query_blocks, keys_blocks, vals_blocks, to_blocks(grad_mixed), log_norm)
    )
    grad_query = grad_query.reshape(group_rows, local_width)
    grad_keys = grad_keys.reshape(group_rows, local_width)
    grad_vals = grad_vals.reshape(group_rows, local_width)
    grad_head = jnp.stack([jnp.sum(grad_query, axis=0), jnp.sum(grad_vals, axis=0)])
    grad_proj = jnp.stack([grad_query, grad_keys, grad_vals]).astype(jnp.bfloat16)
    grad_qkv = jnp.einsum("rd,irk->idk", first_in, grad_proj, preferred_element_type=jnp.float32)
    grad_first = lax.psum_scatter(
        jnp.einsum("irk,idk->rd", grad_proj, qkv_full, preferred_element_type=jnp.float32).astype(
            jnp.bfloat16
        ),
        "tensor",
        scatter_dimension=0,
        tiled=True,
    ).astype(jnp.float32)
    gain_one = jnp.sum(grad_first * normed_one, axis=0)
    shift_one = jnp.sum(grad_first, axis=0)
    grad_tokens = grad_hidden + norm_back(grad_first, normed_one, spread_one, gain_rows[0])
    grad_head_all, grad_fc1_bias_all = lax.psum((grad_head, grad_fc1_bias), "dp")
    grad_qkv_own, grad_out_own, grad_fc1_own, grad_fc2_own = (
        lax.psum_scatter(
            grad_qkv.astype(jnp.bfloat16), "dp", scatter_dimension=1, tiled=True
        ).astype(jnp.float32),
        lax.psum_scatter(
            grad_wout.astype(jnp.bfloat16), "dp", scatter_dimension=1, tiled=True
        ).astype(jnp.float32),
        lax.psum_scatter(
            grad_fc1.astype(jnp.bfloat16), "dp", scatter_dimension=0, tiled=True
        ).astype(jnp.float32),
        lax.psum_scatter(
            grad_fc2.astype(jnp.bfloat16), "dp", scatter_dimension=1, tiled=True
        ).astype(jnp.float32),
    )
    grad_gains_own, grad_shifts_own = (
        lax.psum_scatter(
            jnp.stack([gain_one, gain_two]), ("dp", "tensor"), scatter_dimension=1, tiled=True
        ),
        lax.psum_scatter(
            jnp.stack([shift_one, shift_out, shift_two, shift_fc2]),
            ("dp", "tensor"),
            scatter_dimension=1,
            tiled=True,
        ),
    )
    return (
        output,
        grad_tokens,
        grad_gains_own,
        grad_shifts_own,
        grad_qkv_own,
        grad_head_all,
        grad_out_own,
        grad_fc1_own,
        grad_fc1_bias_all,
        grad_fc2_own,
    )


def solution(mesh):
    in_specs = (
        P(("dp", "tensor"), None),
        P(None, ("dp", "tensor")),
        P(None, ("dp", "tensor")),
        P(None, "dp", "tensor"),
        P(None, "tensor"),
        P("tensor", "dp"),
        P("dp", "tensor"),
        P("tensor"),
        P("tensor", "dp"),
        P(("dp", "tensor"), None),
    )
    out_specs = (
        P(("dp", "tensor"), None),
        P(("dp", "tensor"), None),
        P(None, ("dp", "tensor")),
        P(None, ("dp", "tensor")),
        P(None, "dp", "tensor"),
        P(None, "tensor"),
        P("tensor", "dp"),
        P("dp", "tensor"),
        P("tensor"),
        P("tensor", "dp"),
    )
    return jax.shard_map(body, mesh=mesh, in_specs=in_specs, out_specs=out_specs, check_vma=False)
```

profile of v0, /device:TPU:0, one launch (start us, length us, event | category | flops | bytes accessed | tf_op | source)
XLA Modules:
  0.0 974.4 jit_solution(12943085000319028319)
XLA Ops:
  8.0 71.1 %all-gather = f32[32,36,2]{1,2,0:T(2,128)S(1)} all-gather(f32[1,36,2]{1,2,0:T(2,128)} %bitcast.180), channel_id=1, replica_groups=mesh['dp'=8,'tensor'=4] {'dp','tensor'}, dimensions={0}, use_global_device_ids=true | all-gather | bytes 9504 | tf_op jit(solution)/shard_map/all_gather | solution.py:73
  79.2 63.9 %all-gather.1 = f32[32,36,4]{1,2,0:T(4,128)S(1)} all-gather(f32[1,36,4]{1,2,0:T(4,128)} %bitcast.179), channel_id=1, replica_groups=mesh['dp'=8,'tensor'=4] {'dp','tensor'}, dimensions={0}, use_global_device_ids=true | all-gather | bytes 19008 | tf_op jit(solution)/shard_map/all_gather | solution.py:74
  148.2 16.7 %all_gather.34 = bf16[288,1152]{0,1:T(8,128)(2,1)} all-gather(bf16[288,144]{0,1:T(8,128)(2,1)S(1)} %copy-done.11), channel_id=1, replica_groups=mesh['dp'=8,'tensor'=4] {'dp'}, dimensions={1}, use_global_device_ids=true | all-gather | bytes 746496 | tf_op jit(solution)/shard_map/all_gather | solution.py:78
  164.8 37.7 %all-gather.10.cloned.1.call-done = bf16[2048,1152]{1,0:T(8,128)(2,1)} async-done(((bf16[512,1152]{1,0:T(8,128)(2,1)}), bf16[2048,1152]{1,0:T(8,128)(2,1)}) %all-gather.10.cloned.1.call-update) | async-done | bytes 4718608 | tf_op jit(solution)/shard_map/all_gather | solution.py:85
  226.1 15.5 %while.26 = (s32[]{:T(128)}, bf16[4,2,256,4,72]{2,1,0,4,3:T(2,128)(2,1)}, f32[4,2,4,256]{3,2,1,0:T(4,128)}, bf16[4,2,256,4,72]{2,4,3,1,0:T(8,128)(2,1)}, bf16[4,...) while((s32[]{:T(128)}, bf16[4,2,256,4,72]{2,1,0,4,3:T(2,128)(2,1)}, ...), condition=%wide.region_5.6_spmd, body=%wide.region_2.5_spmd.sunk | while | flops 153761792 | bytes 8127585 | solution.py:110
  254.4 55.1 %reduce-scatter.13.cloned.1.call-done = bf16[512,1152]{1,0:T(8,128)(2,1)} async-done(((bf16[2048,1152]{1,0:T(8,128)(2,1)}), bf16[512,1152]{1,0:T(8,128)(2,1)}) %reduce-scatter.13.cloned.1.call-update) | async-done | bytes 1179664 | tf_op jit(solution)/shard_map/reduce_scatter | solution.py:112
  314.3 30.7 %all-gather.18.cloned.1.call-done = bf16[1076,1152]{0,1:T(8,128)(2,1)} async-done(((bf16[1076,144]{0,1:T(8,128)(2,1)}), bf16[1076,1152]{0,1:T(8,128)(2,1)}) %all-gather.18.cloned.1.call-update) | async-done | bytes 2479120 | tf_op jit(solution)/shard_map/all_gather | solution.py:80
  345.0 57.8 %all-gather.20.cloned.1.call-done = bf16[2048,1152]{1,0:T(8,128)(2,1)} async-done(((bf16[512,1152]{1,0:T(8,128)(2,1)}), bf16[2048,1152]{1,0:T(8,128)(2,1)}) %all-gather.20.cloned.1.call-update) | async-done | bytes 4718608 | tf_op jit(solution)/shard_map/all_gather | solution.py:86
  402.8 10.7 %fusion.80 = f32[2048,1076]{0,1:T(8,128)} fusion(bf16[2048,1152]{1,0:T(8,128)(2,1)} %all-gather.20.cloned.1.call-done, bf16[1076,1152]{0,1:T(8,128)(2,1)} %all-gather.18.cloned.1.call-done), kind=kOutput, calls=%fused_computation.147 | convolution fusion | flops 5077204992 | bytes 16012288 | tf_op jit(solution)/shard_map/dot_general | solution.py:133
  413.5 24.8 %all-gather.16.cloned.1.call-done = bf16[1152,1076]{1,0:T(8,128)(2,1)} async-done(((bf16[144,1076]{1,0:T(8,128)(2,1)}), bf16[1152,1076]{1,0:T(8,128)(2,1)}) %all-gather.16.cloned.1.call-update) | async-done | bytes 2479120 | tf_op jit(solution)/shard_map/all_gather | solution.py:79
  438.3 58.5 %all-gather.14.cloned.1.call-done = bf16[2048,1152]{1,0:T(8,128)(2,1)} async-done(((bf16[512,1152]{1,0:T(8,128)(2,1)}), bf16[2048,1152]{1,0:T(8,128)(2,1)}) %all-gather.14.cloned.1.call-update) | async-done | bytes 4718608 | tf_op jit(solution)/shard_map/all_gather | solution.py:120
  496.8 18.4 %fusion.74 = (f32[1076]{0:T(1024)}, bf16[2048,1076]{0,1:T(8,128)(2,1)S(1)}, f32[2048,1076]{0,1:T(8,128)}) fusion(f32[2048,1076]{0,1:T(8,128)} %fusion.80, f32[1076]{0:T(1024)} %param.21, bf16[2048,1152]{1,0:T(8,128)(2,1)} %all-gather.14.cloned.1.call-done, bf16[1152,1076]{1,0:T(8,128)(2,1)} %all-gather.16.cloned.1.call-done), kind=kOutput, calls=%fused_computation.142 | convolution fusion | flops 5125684224 | bytes 29242784 | tf_op jit(solution)/shard_map/dot_general | solution.py:121
  526.4 13.1 %convolution_convert_fusion.4 = bf16[2048,1152]{1,0:T(8,128)(2,1)} fusion(bf16[1076,1152]{0,1:T(8,128)(2,1)} %all-gather.18.cloned.1.call-done, f32[2048,1076]{0,1:T(8,128)} %get-tuple-element.238), kind=kOutput, calls=%fused_computation.60 | convolution fusion | flops 5099397120 | bytes 16012288 | tf_op jit(solution)/shard_map/dot_general | solution.py:125
  539.5 43.9 %reduce-scatter.17.cloned.1.call-done = bf16[512,1152]{1,0:T(8,128)(2,1)} async-done(((bf16[2048,1152]{1,0:T(8,128)(2,1)}), bf16[512,1152]{1,0:T(8,128)(2,1)}) %reduce-scatter.17.cloned.1.call-update) | async-done | bytes 1179664 | tf_op jit(solution)/shard_map/reduce_scatter | solution.py:138
  587.8 55.7 %reduce-scatter.15.cloned.1.call-done = bf16[512,1152]{1,0:T(8,128)(2,1)} async-done(((bf16[2048,1152]{1,0:T(8,128)(2,1)}), bf16[512,1152]{1,0:T(8,128)(2,1)}) %reduce-scatter.15.cloned.1.call-update) | async-done | bytes 1179664 | tf_op jit(solution)/shard_map/reduce_scatter | solution.py:124
  651.1 13.0 %convolution_convert_fusion.1 = bf16[1076,1152]{0,1:T(8,128)(2,1)} fusion(bf16[2048,1152]{1,0:T(8,128)(2,1)} %all-gather.20.cloned.1.call-done, f32[2048,1076]{0,1:T(8,128)} %get-tuple-element.238), kind=kOutput, calls=%fused_computation.57 | convolution fusion | flops 5098277376 | bytes 16012288 | tf_op jit(solution)/shard_map/dot_general | solution.py:132
  664.5 11.6 %convolution_convert_fusion.2 = bf16[1152,1076]{1,0:T(8,128)(2,1)} fusion(bf16[2048,1152]{1,0:T(8,128)(2,1)} %all-gather.14.cloned.1.call-done, bf16[2048,1076]{0,1:T(8,128)(2,1)} %copy-done.33), kind=kOutput, calls=%fused_computation.58 | convolution fusion | flops 5078444544 | bytes 11604992 | tf_op jit(solution)/shard_map/dot_general | solution.py:137
  676.1 31.8 %all-gather.22.cloned.1.call-done = bf16[2048,1152]{1,0:T(8,128)(2,1)} async-done(((bf16[512,1152]{1,0:T(8,128)(2,1)}), bf16[2048,1152]{1,0:T(8,128)(2,1)}) %all-gather.22.cloned.1.call-update) | async-done | bytes 4718608 | tf_op jit(solution)/shard_map/all_gather | solution.py:150
  717.5 29.5 %while.27 = (s32[]{:T(128)}, f32[4,2,256,4,72]{2,4,3,1,0:T(8,128)}, bf16[4,2,256,4,72]{2,4,3,1,0:T(8,128)(2,1)}, f32[4,2,256,4,72]{2,4,3,1,0:T(8,128)}, bf16[4,2...) while((s32[]{:T(128)}, f32[4,2,256,4,72]{2,4,3,1,0:T(8,128)}, ...), condition=%wide.region_15.16_spmd, body=%wide.region_13.15_spmd.sunk | while | flops 381302784 | bytes 29633716 | solution.py:155
  796.2 11.0 %bitcast_convert_fusion = bf16[2048,1152]{1,0:T(8,128)(2,1)} fusion(bf16[3,2048,288]{1,2,0:T(8,128)(2,1)} %constant_dynamic-update-slice_fusion, bf16[3,1152,288]{2,1,0:T(8,128)(2,1)} %all-gather.12.cloned.1.call-done), kind=kOutput, calls=%fused_computation.48 | convolution fusion | flops 4079222784 | bytes 10248192 | tf_op jit(solution)/shard_map/irk,idk->rd/dot_general | solution.py:165
  813.7 28.7 %all-reduce.3 = (f32[2,288]{1,0:T(2,128)}, f32[1076]{0:T(1024)}) all-reduce(f32[2,288]{1,0:T(2,128)S(1)} %pad_maximum_fusion.2, f32[1076]{0:T(1024)S(1)} %copy-done.29), channel_id=1, replica_groups=mesh['dp'=8,'tensor'=4] {'dp'}, use_global_device_ids=true, to_apply=%region_30.31 | all-reduce | flops 1652 | bytes 13216 | tf_op jit(solution)/shard_map/psum | solution.py:175
  844.0 14.2 %reduce-scatter.27.cloned.1.call-done = bf16[144,864]{1,0:T(8,128)(2,1)} async-done(((bf16[1152,864]{1,0:T(8,128)(2,1)}), bf16[144,864]{1,0:T(8,128)(2,1)}) %reduce-scatter.27.cloned.1.call-update) | async-done | bytes 248848
  864.6 51.7 %reduce-scatter.19.cloned.1.call-done = bf16[512,1152]{1,0:T(8,128)(2,1)} async-done(((bf16[2048,1152]{1,0:T(8,128)(2,1)}), bf16[512,1152]{1,0:T(8,128)(2,1)}) %reduce-scatter.19.cloned.1.call-update) | async-done | bytes 1179664 | tf_op jit(solution)/shard_map/reduce_scatter | solution.py:164
  921.2 40.3 %all-reduce.2 = (f32[2,1152]{1,0:T(2,128)}, f32[4,1152]{1,0:T(4,128)}) all-reduce(f32[2,1152]{1,0:T(2,128)} %pad_maximum_fusion.1, f32[4,1152]{1,0:T(4,128)} %pad_maximum_fusion), channel_id=6, replica_groups=mesh['dp'=8,'tensor'=4] {'dp','tensor'}, use_global_device_ids=true, to_apply=%region_21.22.clone | all-reduce | flops 6912 | bytes 55296
  (244 shorter events, 199.3 us)
Async XLA Ops:
  7.2 138.3 %copy-start = (bf16[512,1152]{1,0:T(8,128)(2,1)S(1)}, bf16[512,1152]{1,0:T(8,128)(2,1)}, u32[]{:S(2)}) copy-start(bf16[512,1152]{1,0:T(8,128)(2,1)} %param.14) | copy-start | bytes 3538948
  7.2 157.7 %all-gather.12.cloned.1.call-start = ((), (), s32[]{:S(2)}) async-start(), calls=%async_computation.9 | async-start | bytes 2985984 | tf_op jit(solution)/shard_map/all_gather | solution.py:77
  7.9 194.6 %all-gather.10.cloned.1.call-start = ((), (), s32[]{:S(2)}) async-start(), calls=%async_computation.8 | async-start | bytes 5898240 | tf_op jit(solution)/shard_map/all_gather | solution.py:85
  145.9 56.6 %copy-start.15 = (f32[512]{0:T(512)}, f32[512]{0:T(512)S(1)}, u32[]{:S(2)}) copy-start(f32[512]{0:T(512)S(1)} %add_rsqrt_fusion.1) | copy-start | bytes 6148
  147.5 162.0 %reduce-scatter.13.cloned.1.call-start = ((), (), s32[]{:S(2)}) async-start(), calls=%async_computation.10 | async-start | bytes 5898240 | tf_op jit(solution)/shard_map/reduce_scatter | solution.py:112
  241.6 10.7 %copy-start.2 = (bf16[4,2,256,4,72]{2,4,3,1,0:T(8,128)(2,1)}, bf16[4,2,256,4,72]{2,4,3,1,0:T(8,128)(2,1)S(1)}, u32[]{:S(2)}) copy-start(bf16[4,2,256,4,72]{2,4,3,1,0:T(8,128)(2,1)S(1)} %get-tuple-element.416) | copy-start | bytes 3538948
  252.4 92.6 %all-gather.18.cloned.1.call-start = ((), (), s32[]{:S(2)}) async-start(), calls=%async_computation.13 | async-start | bytes 2985984 | tf_op jit(solution)/shard_map/all_gather | solution.py:80
  252.9 149.8 %all-gather.20.cloned.1.call-start = ((), (), s32[]{:S(2)}) async-start(), calls=%async_computation.15 | async-start | bytes 5898240 | tf_op jit(solution)/shard_map/all_gather | solution.py:86
  253.5 184.7 %all-gather.16.cloned.1.call-start = ((), (), s32[]{:S(2)}) async-start(), calls=%async_computation.12 | async-start | bytes 2985984 | tf_op jit(solution)/shard_map/all_gather | solution.py:79
  254.1 242.7 %all-gather.14.cloned.1.call-start = ((), (), s32[]{:S(2)}) async-start(), calls=%async_computation.11 | async-start | bytes 5898240 | tf_op jit(solution)/shard_map/all_gather | solution.py:120
  314.3 269.2 %reduce-scatter.17.cloned.1.call-start = ((), (), s32[]{:S(2)}) async-start(), calls=%async_computation.16 | async-start | bytes 5898240 | tf_op jit(solution)/shard_map/reduce_scatter | solution.py:138
  496.8 20.4 %copy-start.32 = (bf16[1152,1076]{1,0:T(8,128)(2,1)S(1)}, bf16[1152,1076]{1,0:T(8,128)(2,1)}, u32[]{:S(2)}) copy-start(bf16[1152,1076]{1,0:T(8,128)(2,1)} %all-gather.16.cloned.1.call-done) | copy-start | bytes 7437316
  526.3 117.1 %reduce-scatter.15.cloned.1.call-start = ((), (), s32[]{:S(2)}) async-start(), calls=%async_computation.14 | async-start | bytes 5898240 | tf_op jit(solution)/shard_map/reduce_scatter | solution.py:124
  539.5 168.5 %all-gather.22.cloned.1.call-start = ((), (), s32[]{:S(2)}) async-start(), calls=%async_computation.17 | async-start | bytes 5898240 | tf_op jit(solution)/shard_map/all_gather | solution.py:150
  650.9 156.4 %reduce-scatter.25.cloned.1.call-start = ((), (), s32[]{:S(2)}) async-start(), calls=%async_computation.21 | async-start | bytes 2985984 | tf_op jit(solution)/shard_map/reduce_scatter | solution.py:186
  664.2 145.0 %reduce-scatter.23.cloned.1.call-start = ((), (), s32[]{:S(2)}) async-start(), calls=%async_computation.20 | async-start | bytes 2985984 | tf_op jit(solution)/shard_map/reduce_scatter | solution.py:183
  676.1 31.9 %copy-start.8 = (bf16[288,1152]{0,1:T(8,128)(2,1)S(1)}, bf16[288,1152]{0,1:T(8,128)(2,1)}, u32[]{:S(2)}) copy-start(bf16[288,1152]{0,1:T(8,128)(2,1)} %all_gather.34) | copy-start | bytes 1990660
  676.1 166.3 %reduce-scatter.21.cloned.1.call-start = ((), (), s32[]{:S(2)}) async-start(), calls=%async_computation.19 | async-start | bytes 995328 | tf_op jit(solution)/shard_map/reduce_scatter | solution.py:180
  769.4 88.8 %reduce-scatter.27.cloned.1.call-start = ((), (), s32[]{:S(2)}) async-start(), calls=%async_computation.22 | async-start | bytes 2322432
  796.2 120.2 %reduce-scatter.19.cloned.1.call-start = ((), (), s32[]{:S(2)}) async-start(), calls=%async_computation.18 | async-start | bytes 5898240 | tf_op jit(solution)/shard_map/reduce_scatter | solution.py:164
  807.3 109.1 %copy-start.10 = (f32[1152]{0:T(1024)S(1)}, f32[1152]{0:T(1024)}, u32[]{:S(2)}) copy-start(f32[1152]{0:T(1024)} %copy-done.9) | copy-start | bytes 13828
  807.3 109.1 %copy-start.13 = (f32[512]{0:T(512)S(1)}, f32[512]{0:T(512)}, u32[]{:S(2)}) copy-start(f32[512]{0:T(512)} %copy-done.12) | copy-start | bytes 6148
  807.3 109.0 %copy-start.16 = (f32[512]{0:T(512)S(1)}, f32[512]{0:T(512)}, u32[]{:S(2)}) copy-start(f32[512]{0:T(512)} %copy-done.15) | copy-start | bytes 6148
  860.4 103.8 %copy-start.5 = (f32[512,1152]{1,0:T(8,128)S(1)}, f32[512,1152]{1,0:T(8,128)}, u32[]{:S(2)}) copy-start(f32[512,1152]{1,0:T(8,128)} %copy-done.4) | copy-start | bytes 7077892
  (31 other events, 90.1 us)
Sparse Core Ops, SparseCore 0:
  9.6 36.7 all-gather.11
  147.6 54.8 all-gather.9
  252.5 56.9 reduce-scatter.12
  311.0 33.9 all-gather.17
  346.7 56.0 all-gather.19
  404.3 33.9 all-gather.15
  440.7 56.0 all-gather.13
  526.4 56.9 reduce-scatter.16
  586.4 56.9 reduce-scatter.14
  651.0 56.8 all-gather.21
  710.3 38.0 reduce-scatter.24
  750.5 37.2 reduce-scatter.22
  790.1 31.4 reduce-scatter.20
  823.7 34.3 reduce-scatter.26
  861.0 55.2 reduce-scatter.18
where the time goes:
time: 980 us; the launch traced here: 974 us
  waiting for transfers between devices  464 us (47%)
  blocking collectives  221 us (23%)
  matrix products  155 us (16%)
  local copies, waits for them, and re-layouts  75 us (8%)
  other arithmetic  43 us (4%)
  between operations  14.5 us (1%)
    all_gather x1, blocking collectives, body(): lax.all_gather(norm_gains, ('dp', 'tensor'), axis=1, tiled=True)  71.1 us
    all_gather x1, blocking collectives, body(): lax.all_gather(row_biases, ('dp', 'tensor'), axis=1, tiled=True)  63.9 us
    all_gather x1, waiting for transfers between devices, body(): lax.all_gather(second_f.astype(jnp.bfloat16), 'tensor', axis=0, tiled=True)  58.5 us
    all_gather x1, waiting for transfers between devices, body(): lax.all_gather(cotangent, 'tensor', axis=0, tiled=True)  57.8 us
    reduce_scatter x1, waiting for transfers between devices, body(): lax.psum_scatter(jnp.dot(act_in, fc2_full, preferred_element_type=jnp.flo...  55.7 us
    reduce_scatter x1, waiting for transfers between devices, body(): lax.psum_scatter(jnp.dot(mixed, out_full, preferred_element_type=jnp.floa...  55.1 us
    reduce_scatter x1, waiting for transfers between devices, body(): lax.psum_scatter(jnp.einsum('irk,idk->rd', grad_proj, qkv_full, preferred...  51.7 us
    reduce_scatter x1, waiting for transfers between devices, body(): lax.psum_scatter(jnp.dot(grad_pre_in, fc1_full.T, preferred_element_type=...  43.9 us
  transfers between devices with their start and end apart: 15, of which 11 were waited for; matrix products, arithmetic and copies ran while one was open for 18% of the time, Pallas kernels for 0%

commit v1 on v0

--- a/solution.py
+++ b/solution.py
@@ -6,6 +6,28 @@
 HD = 72
 SEQ = 256
 EPS = 1e-06
+
+
+def in_order(parts, dim):
+    lengths = list(parts.shape[1:])
+    lengths[dim] *= parts.shape[0]
+    return jnp.moveaxis(parts, 0, dim).reshape(lengths)
+
+
+def collect(array, axis, dim):
+    size = lax.axis_size(axis)
+    pairs = [(i, (i + 1) % size) for i in range(size)]
+    back = [(b, a) for a, b in pairs]
+    lower, upper = ([], [])
+    for step in range(size - 1):
+        if step % 2 == 0:
+            lower.append(lax.ppermute(lower[-1] if lower else array, axis, pairs))
+        else:
+            upper.append(lax.ppermute(upper[-1] if upper else array, axis, back))
+    tiles = jnp.stack([*lower[::-1], array, *upper])
+    shift = lax.axis_index(axis) - len(lower)
+    tiles = tiles[(jnp.arange(size) - shift) % size]
+    return in_order(tiles, dim)
 
 
 def norm_rows(values, gain_row, shifts):
@@ -83,7 +105,7 @@
     first_f, normed_one, spread_one = norm_rows(inputs_f, gain_rows[0], shifts[0])
     first_in, cot_all = (
         lax.all_gather(first_f.astype(jnp.bfloat16), "tensor", axis=0, tiled=True),
-        lax.all_gather(cotangent, "tensor", axis=0, tiled=True),
+        collect(cotangent, "tensor", 0),
     )
     group_rows = first_in.shape[0]
     images = group_rows // SEQ

time: 980 us -> 948 us (0.967)
  waiting for transfers between devices: 464 us -> 420 us
    ppermute x0 -> x3, waiting for transfers between devices: none -> 104 us  [the longest x2 67.6 us: collect(): lower.append(lax.ppermute(lower[-1] if lower else array, axis, pairs))]
    all_gather x1, waiting for transfers between devices: 58.5 us -> 0.01 us  [body(): lax.all_gather(second_f.astype(jnp.bfloat16), 'tensor', axis=0, tiled=True)]
    all_gather x1 -> x0, waiting for transfers between devices: 57.8 us -> none  [body(): lax.all_gather(cotangent, 'tensor', axis=0, tiled=True)]
    all_gather x1, waiting for transfers between devices: 24.8 us -> 0.01 us  [body(): lax.all_gather(w_fc1, 'dp', axis=0, tiled=True)]
  transfers between devices with their start and end apart: 15 -> 17, of which waited for: 11 -> 11; matrix products, arithmetic and copies ran while one was open for 18% -> 20% of each run, Pallas kernels for 0% -> 0%
where the time goes in v1:
time: 948 us; the launch traced here: 943 us
  waiting for transfers between devices  420 us (44%)
  blocking collectives  221 us (23%)
  matrix products  154 us (16%)
  local copies, waits for them, and re-layouts  80.7 us (9%)
  other arithmetic  47.7 us (5%)
  between operations  14.5 us (2%)
    all_gather x1, blocking collectives, body(): lax.all_gather(norm_gains, ('dp', 'tensor'), axis=1, tiled=True)  71.1 us
    ppermute x2, waiting for transfers between devices, collect(): lower.append(lax.ppermute(lower[-1] if lower else array, axis, pairs))  67.6 us
    all_gather x1, blocking collectives, body(): lax.all_gather(row_biases, ('dp', 'tensor'), axis=1, tiled=True)  63.9 us
    reduce_scatter x1, waiting for transfers between devices, body(): lax.psum_scatter(jnp.dot(mixed, out_full, preferred_element_type=jnp.floa...  56.3 us
    reduce_scatter x1, waiting for transfers between devices, body(): lax.psum_scatter(jnp.dot(act_in, fc2_full, preferred_element_type=jnp.flo...  55.6 us
    reduce_scatter x1, waiting for transfers between devices, body(): lax.psum_scatter(jnp.einsum('irk,idk->rd', grad_proj, qkv_full, preferred...  51.9 us
    reduce_scatter x1, waiting for transfers between devices, body(): lax.psum_scatter(jnp.dot(grad_pre_in, fc1_full.T, preferred_element_type=...  43 us
    unnamed x1, blocking collectives  40.3 us
  transfers between devices with their start and end apart: 17, of which 11 were waited for; matrix products, arithmetic and copies ran while one was open for 20% of the time, Pallas kernels for 0%

profile of v1, /device:TPU:0, one launch (start us, length us, event | category | flops | bytes accessed | tf_op | source)
XLA Modules:
  0.0 942.9 jit_solution(15672947329592630429)
XLA Ops:
  8.0 71.1 %all-gather = f32[32,36,2]{1,2,0:T(2,128)S(1)} all-gather(f32[1,36,2]{1,2,0:T(2,128)} %bitcast.190), channel_id=1, replica_groups=mesh['dp'=8,'tensor'=4] {'dp','tensor'}, dimensions={0}, use_global_device_ids=true | all-gather | bytes 9504 | tf_op jit(solution)/shard_map/all_gather | solution.py:95
  79.2 63.9 %all-gather.1 = f32[32,36,4]{1,2,0:T(4,128)S(1)} all-gather(f32[1,36,4]{1,2,0:T(4,128)} %bitcast.189), channel_id=1, replica_groups=mesh['dp'=8,'tensor'=4] {'dp','tensor'}, dimensions={0}, use_global_device_ids=true | all-gather | bytes 19008 | tf_op jit(solution)/shard_map/all_gather | solution.py:96
  148.2 16.7 %all_gather.31 = bf16[288,1152]{0,1:T(8,128)(2,1)} all-gather(bf16[288,144]{0,1:T(8,128)(2,1)S(1)} %copy-done.11), channel_id=1, replica_groups=mesh['dp'=8,'tensor'=4] {'dp'}, dimensions={1}, use_global_device_ids=true | all-gather | bytes 746496 | tf_op jit(solution)/shard_map/all_gather | solution.py:100
  164.8 37.7 %all-gather.9.cloned.1.call-done = bf16[2048,1152]{1,0:T(8,128)(2,1)} async-done(((bf16[512,1152]{1,0:T(8,128)(2,1)}), bf16[2048,1152]{1,0:T(8,128)(2,1)}) %all-gather.9.cloned.1.call-update) | async-done | bytes 4718608 | tf_op jit(solution)/shard_map/all_gather | solution.py:107
  226.1 15.5 %while.26 = (s32[]{:T(128)}, bf16[4,2,256,4,72]{2,1,0,4,3:T(2,128)(2,1)}, f32[4,2,4,256]{3,2,1,0:T(4,128)}, bf16[4,2,256,4,72]{2,4,3,1,0:T(8,128)(2,1)}, bf16[4,...) while((s32[]{:T(128)}, bf16[4,2,256,4,72]{2,1,0,4,3:T(2,128)(2,1)}, ...), condition=%wide.region_5.6_spmd, body=%wide.region_2.5_spmd.sunk | while | flops 153761792 | bytes 8127585 | solution.py:132
  253.2 56.3 %reduce-scatter.13.cloned.1.call-done = bf16[512,1152]{1,0:T(8,128)(2,1)} async-done(((bf16[2048,1152]{1,0:T(8,128)(2,1)}), bf16[512,1152]{1,0:T(8,128)(2,1)}) %reduce-scatter.13.cloned.1.call-update) | async-done | bytes 1179664 | tf_op jit(solution)/shard_map/reduce_scatter | solution.py:134
  317.4 27.0 %collective-permute-done = bf16[512,1152]{1,0:T(8,128)(2,1)} collective-permute-done((bf16[512,1152]{1,0:T(8,128)(2,1)}, bf16[512,1152]{1,0:T(8,128)(2,1)}, u32[]{:S(2)}, u32[]{:S(2)}) %collective-permute-start) | collective-permute-done | bytes 1179680 | tf_op jit(solution)/shard_map/ppermute | solution.py:24
  345.6 36.6 %collective-permute-done.2 = bf16[512,1152]{1,0:T(8,128)(2,1)} collective-permute-done((bf16[512,1152]{1,0:T(8,128)(2,1)}, bf16[512,1152]{1,0:T(8,128)(2,1)}, u32[]{:S(2)}, u32[]{:S(2)}) %collective-permute-start.2) | collective-permute-done | bytes 1179680 | tf_op jit(solution)/shard_map/ppermute | solution.py:26
  382.2 40.6 %collective-permute-done.1 = bf16[512,1152]{1,0:T(8,128)(2,1)} collective-permute-done((bf16[512,1152]{1,0:T(8,128)(2,1)}, bf16[512,1152]{1,0:T(8,128)(2,1)}, u32[]{:S(2)}, u32[]{:S(2)}) %collective-permute-start.1) | collective-permute-done | bytes 1179680 | tf_op jit(solution)/shard_map/ppermute | solution.py:24
  432.7 10.7 %convolution_add_fusion = f32[2048,1076]{0,1:T(8,128)} fusion(bf16[2048,1152]{1,0:T(8,128)(2,1)} %all-gather.13.cloned.1.call-done, bf16[1152,1076]{1,0:T(8,128)(2,1)} %all-gather.15.cloned.1.call-done, f32[1076]{0:T(1024)} %param.21), kind=kOutput, calls=%fused_computation.50 | convolution fusion | flops 5079408640 | bytes 16016592 | tf_op jit(solution)/shard_map/dot_general | solution.py:143
  443.4 23.9 %all-gather.17.cloned.1.call-done = bf16[1076,1152]{0,1:T(8,128)(2,1)} async-done(((bf16[1076,144]{0,1:T(8,128)(2,1)}), bf16[1076,1152]{0,1:T(8,128)(2,1)}) %all-gather.17.cloned.1.call-update) | async-done | bytes 2479120 | tf_op jit(solution)/shard_map/all_gather | solution.py:102
  467.3 17.0 %fusion.76 = (f32[1076]{0:T(1024)}, bf16[2048,1076]{0,1:T(8,128)(2,1)S(1)}) fusion(f32[2048,1076]{0,1:T(8,128)} %convolution_add_fusion, bf16[2048,1152]{1,0:T(8,128)(2,1)} %bitcast.184, bf16[1076,1152]{0,1:T(8,128)(2,1)} %all-gather.17.cloned.1.call-done), kind=kOutput, calls=%fused_computation.151 | convolution fusion | flops 5123480576 | bytes 20423888 | tf_op jit(solution)/shard_map/dot_general | solution.py:155
  495.6 13.1 %convolution_convert_fusion.4 = bf16[2048,1152]{1,0:T(8,128)(2,1)} fusion(bf16[1076,1152]{0,1:T(8,128)(2,1)} %all-gather.17.cloned.1.call-done, f32[2048,1076]{0,1:T(8,128)} %convolution_add_fusion), kind=kOutput, calls=%fused_computation.61 | convolution fusion | flops 5099397120 | bytes 16012288 | tf_op jit(solution)/shard_map/dot_general | solution.py:147
  508.8 43.0 %reduce-scatter.17.cloned.1.call-done = bf16[512,1152]{1,0:T(8,128)(2,1)} async-done(((bf16[2048,1152]{1,0:T(8,128)(2,1)}), bf16[512,1152]{1,0:T(8,128)(2,1)}) %reduce-scatter.17.cloned.1.call-update) | async-done | bytes 1179664 | tf_op jit(solution)/shard_map/reduce_scatter | solution.py:160
  556.2 55.6 %reduce-scatter.15.cloned.1.call-done = bf16[512,1152]{1,0:T(8,128)(2,1)} async-done(((bf16[2048,1152]{1,0:T(8,128)(2,1)}), bf16[512,1152]{1,0:T(8,128)(2,1)}) %reduce-scatter.15.cloned.1.call-update) | async-done | bytes 1179664 | tf_op jit(solution)/shard_map/reduce_scatter | solution.py:146
  619.5 13.0 %convolution_convert_fusion.1 = bf16[1076,1152]{0,1:T(8,128)(2,1)} fusion(bf16[2048,1152]{1,0:T(8,128)(2,1)} %bitcast.185, f32[2048,1076]{0,1:T(8,128)} %convolution_add_fusion), kind=kOutput, calls=%fused_computation.58 | convolution fusion | flops 5098277376 | bytes 16012288 | tf_op jit(solution)/shard_map/dot_general | solution.py:154
  632.8 11.6 %convolution_convert_fusion.2 = bf16[1152,1076]{1,0:T(8,128)(2,1)} fusion(bf16[2048,1152]{1,0:T(8,128)(2,1)} %all-gather.13.cloned.1.call-done, bf16[2048,1076]{0,1:T(8,128)(2,1)} %copy-done.33), kind=kOutput, calls=%fused_computation.59 | convolution fusion | flops 5078444544 | bytes 11604992 | tf_op jit(solution)/shard_map/dot_general | solution.py:159
  644.5 31.9 %all-gather.19.cloned.1.call-done = bf16[2048,1152]{1,0:T(8,128)(2,1)} async-done(((bf16[512,1152]{1,0:T(8,128)(2,1)}), bf16[2048,1152]{1,0:T(8,128)(2,1)}) %all-gather.19.cloned.1.call-update) | async-done | bytes 4718608 | tf_op jit(solution)/shard_map/all_gather | solution.py:172
  685.8 29.5 %while.27 = (s32[]{:T(128)}, f32[4,2,256,4,72]{2,4,3,1,0:T(8,128)}, bf16[4,2,256,4,72]{2,4,3,1,0:T(8,128)(2,1)}, f32[4,2,256,4,72]{2,4,3,1,0:T(8,128)}, bf16[4,2...) while((s32[]{:T(128)}, f32[4,2,256,4,72]{2,4,3,1,0:T(8,128)}, ...), condition=%wide.region_15.16_spmd, body=%wide.region_13.15_spmd.sunk | while | flops 381302784 | bytes 29633716 | solution.py:177
  764.6 11.0 %bitcast_convert_fusion = bf16[2048,1152]{1,0:T(8,128)(2,1)} fusion(bf16[3,2048,288]{1,2,0:T(8,128)(2,1)} %constant_dynamic-update-slice_fusion, bf16[3,1152,288]{2,1,0:T(8,128)(2,1)} %all-gather.11.cloned.1.call-done), kind=kOutput, calls=%fused_computation.49 | convolution fusion | flops 4079222784 | bytes 10248192 | tf_op jit(solution)/shard_map/irk,idk->rd/dot_general | solution.py:187
  782.0 28.7 %all-reduce.3 = (f32[2,288]{1,0:T(2,128)}, f32[1076]{0:T(1024)}) all-reduce(f32[2,288]{1,0:T(2,128)S(1)} %pad_maximum_fusion.3, f32[1076]{0:T(1024)S(1)} %copy-done.29), channel_id=1, replica_groups=mesh['dp'=8,'tensor'=4] {'dp'}, use_global_device_ids=true, to_apply=%region_30.31 | all-reduce | flops 1652 | bytes 13216 | tf_op jit(solution)/shard_map/psum | solution.py:197
  812.3 14.2 %reduce-scatter.27.cloned.1.call-done = bf16[144,864]{1,0:T(8,128)(2,1)} async-done(((bf16[1152,864]{1,0:T(8,128)(2,1)}), bf16[144,864]{1,0:T(8,128)(2,1)}) %reduce-scatter.27.cloned.1.call-update) | async-done | bytes 248848
  832.9 51.9 %reduce-scatter.19.cloned.1.call-done = bf16[512,1152]{1,0:T(8,128)(2,1)} async-done(((bf16[2048,1152]{1,0:T(8,128)(2,1)}), bf16[512,1152]{1,0:T(8,128)(2,1)}) %reduce-scatter.19.cloned.1.call-update) | async-done | bytes 1179664 | tf_op jit(solution)/shard_map/reduce_scatter | solution.py:186
  889.7 40.3 %all-reduce.2 = (f32[2,1152]{1,0:T(2,128)}, f32[4,1152]{1,0:T(4,128)}) all-reduce(f32[2,1152]{1,0:T(2,128)} %pad_maximum_fusion.2, f32[4,1152]{1,0:T(4,128)} %pad_maximum_fusion.1), channel_id=6, replica_groups=mesh['dp'=8,'tensor'=4] {'dp','tensor'}, use_global_device_ids=true, to_apply=%region_21.22.clone | all-reduce | flops 6912 | bytes 55296
  (251 shorter events, 212.2 us)
Async XLA Ops:
  7.2 138.3 %copy-start = (bf16[512,1152]{1,0:T(8,128)(2,1)S(1)}, bf16[512,1152]{1,0:T(8,128)(2,1)}, u32[]{:S(2)}) copy-start(bf16[512,1152]{1,0:T(8,128)(2,1)} %param.14) | copy-start | bytes 3538948
  7.2 157.7 %all-gather.11.cloned.1.call-start = ((), (), s32[]{:S(2)}) async-start(), calls=%async_computation.9 | async-start | bytes 2985984 | tf_op jit(solution)/shard_map/all_gather | solution.py:99
  7.9 194.6 %all-gather.9.cloned.1.call-start = ((), (), s32[]{:S(2)}) async-start(), calls=%async_computation.8 | async-start | bytes 5898240 | tf_op jit(solution)/shard_map/all_gather | solution.py:107
  145.9 56.6 %copy-start.15 = (f32[512]{0:T(512)}, f32[512]{0:T(512)S(1)}, u32[]{:S(2)}) copy-start(f32[512]{0:T(512)S(1)} %add_rsqrt_fusion.1) | copy-start | bytes 6148
  147.5 162.0 %reduce-scatter.13.cloned.1.call-start = ((), (), s32[]{:S(2)}) async-start(), calls=%async_computation.10 | async-start | bytes 5898240 | tf_op jit(solution)/shard_map/reduce_scatter | solution.py:134
  252.4 180.3 %all-gather.15.cloned.1.call-start = ((), (), s32[]{:S(2)}) async-start(), calls=%async_computation.12 | async-start | bytes 2985984 | tf_op jit(solution)/shard_map/all_gather | solution.py:101
  252.9 179.8 %all-gather.13.cloned.1.call-start = ((), (), s32[]{:S(2)}) async-start(), calls=%async_computation.11 | async-start | bytes 5898240 | tf_op jit(solution)/shard_map/all_gather | solution.py:142
  314.3 153.0 %all-gather.17.cloned.1.call-start = ((), (), s32[]{:S(2)}) async-start(), calls=%async_computation.13 | async-start | bytes 2985984 | tf_op jit(solution)/shard_map/all_gather | solution.py:102
  314.3 30.1 %collective-permute-start = (bf16[512,1152]{1,0:T(8,128)(2,1)}, bf16[512,1152]{1,0:T(8,128)(2,1)}, u32[]{:S(2)}, u32[]{:S(2)}) collective-permute-start(bf16[512,1152]{1,0:T(8,128)(2,1)} %param.23), channel_id=1, source_target_pairs={{0,1},{1,2},{2,3},{3,0},{4,5},{5,6},{6,7},{7,4},{8,9},{9,10},{10,1... | collective-permute-start | bytes 3538952 | tf_op jit(solution)/shard_map/ppermute | solution.py:24
  315.9 235.9 %reduce-scatter.17.cloned.1.call-start = ((), (), s32[]{:S(2)}) async-start(), calls=%async_computation.15 | async-start | bytes 5898240 | tf_op jit(solution)/shard_map/reduce_scatter | solution.py:160
  315.9 66.3 %collective-permute-start.2 = (bf16[512,1152]{1,0:T(8,128)(2,1)}, bf16[512,1152]{1,0:T(8,128)(2,1)}, u32[]{:S(2)}, u32[]{:S(2)}) collective-permute-start(bf16[512,1152]{1,0:T(8,128)(2,1)} %param.23), channel_id=1, source_target_pairs={{1,0},{2,1},{3,2},{0,3},{5,4},{6,5},{7,6},{4,7},{9,8},{10,9},{11,1... | collective-permute-start | bytes 3538952 | tf_op jit(solution)/shard_map/ppermute | solution.py:26
  344.4 78.5 %collective-permute-start.1 = (bf16[512,1152]{1,0:T(8,128)(2,1)}, bf16[512,1152]{1,0:T(8,128)(2,1)}, u32[]{:S(2)}, u32[]{:S(2)}) collective-permute-start(bf16[512,1152]{1,0:T(8,128)(2,1)} %collective-permute-done), channel_id=1, source_target_pairs={{0,1},{1,2},{2,3},{3,0},{4,5},{5,6},{6,7},{7,4},{8,9},{9,10},{10,1... | collective-permute-start | bytes 3538952 | tf_op jit(solution)/shard_map/ppermute | solution.py:24
  495.5 116.2 %reduce-scatter.15.cloned.1.call-start = ((), (), s32[]{:S(2)}) async-start(), calls=%async_computation.14 | async-start | bytes 5898240 | tf_op jit(solution)/shard_map/reduce_scatter | solution.py:146
  508.7 167.6 %all-gather.19.cloned.1.call-start = ((), (), s32[]{:S(2)}) async-start(), calls=%async_computation.16 | async-start | bytes 5898240 | tf_op jit(solution)/shard_map/all_gather | solution.py:172
  619.2 156.5 %reduce-scatter.25.cloned.1.call-start = ((), (), s32[]{:S(2)}) async-start(), calls=%async_computation.20 | async-start | bytes 2985984 | tf_op jit(solution)/shard_map/reduce_scatter | solution.py:208
  632.5 145.1 %reduce-scatter.23.cloned.1.call-start = ((), (), s32[]{:S(2)}) async-start(), calls=%async_computation.19 | async-start | bytes 2985984 | tf_op jit(solution)/shard_map/reduce_scatter | solution.py:205
  644.4 32.0 %copy-start.8 = (bf16[288,1152]{0,1:T(8,128)(2,1)S(1)}, bf16[288,1152]{0,1:T(8,128)(2,1)}, u32[]{:S(2)}) copy-start(bf16[288,1152]{0,1:T(8,128)(2,1)} %all_gather.31) | copy-start | bytes 1990660
  644.4 166.3 %reduce-scatter.21.cloned.1.call-start = ((), (), s32[]{:S(2)}) async-start(), calls=%async_computation.18 | async-start | bytes 995328 | tf_op jit(solution)/shard_map/reduce_scatter | solution.py:202
  737.8 88.7 %reduce-scatter.27.cloned.1.call-start = ((), (), s32[]{:S(2)}) async-start(), calls=%async_computation.21 | async-start | bytes 2322432
  764.5 120.4 %reduce-scatter.19.cloned.1.call-start = ((), (), s32[]{:S(2)}) async-start(), calls=%async_computation.17 | async-start | bytes 5898240 | tf_op jit(solution)/shard_map/reduce_scatter | solution.py:186
  775.6 109.2 %copy-start.10 = (f32[1152]{0:T(1024)S(1)}, f32[1152]{0:T(1024)}, u32[]{:S(2)}) copy-start(f32[1152]{0:T(1024)} %copy-done.9) | copy-start | bytes 13828
  775.7 109.2 %copy-start.13 = (f32[512]{0:T(512)S(1)}, f32[512]{0:T(512)}, u32[]{:S(2)}) copy-start(f32[512]{0:T(512)} %copy-done.12) | copy-start | bytes 6148
  775.7 109.2 %copy-start.16 = (f32[512]{0:T(512)S(1)}, f32[512]{0:T(512)}, u32[]{:S(2)}) copy-start(f32[512]{0:T(512)} %copy-done.15) | copy-start | bytes 6148
  828.7 104.0 %copy-start.5 = (f32[512,1152]{1,0:T(8,128)S(1)}, f32[512,1152]{1,0:T(8,128)}, u32[]{:S(2)}) copy-start(f32[512,1152]{1,0:T(8,128)} %copy-done.4) | copy-start | bytes 7077892
  (33 other events, 119.9 us)
Sparse Core Ops, SparseCore 0:
  9.6 36.7 all-gather.10
  147.6 54.8 all-gather.8
  252.5 56.9 reduce-scatter.12
  311.0 33.9 all-gather.14
  347.2 84.5 all-gather.12
  433.3 33.9 all-gather.16
  495.7 56.0 reduce-scatter.16
  554.8 56.9 reduce-scatter.14
  619.4 56.9 all-gather.18
  678.5 38.0 reduce-scatter.24
  718.9 37.3 reduce-scatter.22
  758.4 31.2 reduce-scatter.20
  792.0 34.4 reduce-scatter.26
  829.3 55.4 reduce-scatter.18
